TPU v7x, 128 devices: a whole 4x4x4 slice. The times are simulated.
128 devices in a mesh: dp: 8 (over y, z_lo), mp: 16 (over x, z_hi, core).
Axes of the slice: x: 4, y: 4, z: 4 (z_hi: 2, z_lo: 2; z = z_hi * 2 + z_lo), core: 2. Of those that a mesh axis runs over, the one named last changes fastest.
Arguments:
- tokens: bfloat16 [8192, 8192], P(('dp', 'mp')), may hold values from -6 to 6
- row_counts: int32 [8, 16], replicated, may hold values from 8 to 64, as said below
- gate_blocks: bfloat16 [64, 16, 128, 256], P('mp'), may hold values from -0.125 to 0.125
- gate_index: int32 [64, 16], P('mp'), may hold values from 0 to 63, as said below
- up_blocks: bfloat16 [64, 16, 128, 256], P('mp'), may hold values from -0.125 to 0.125
- up_index: int32 [64, 16], P('mp'), may hold values from 0 to 63, as said below
- down_blocks: bfloat16 [64, 16, 256, 128], P('mp'), may hold values from -0.09375 to 0.09375
- down_index: int32 [64, 16], P('mp'), may hold values from 0 to 63, as said below
Outputs:
- layer_out: bfloat16 [8192, 8192], P(('dp', 'mp'))
Inputs may be any that keep to these rules, and one draw needn't show every extreme that they name: `row_counts`: every entry is a multiple of 8; the entries of one column (one mp index) add up to 32 times the number of dp indices, and every column holds one entry equal to 64. `gate_index`: each row holds 16 distinct block rows in increasing order. `up_index`: each row holds 16 distinct block rows in increasing order. `down_index`: each row holds 16 distinct block columns in increasing order.
All inputs are finite; a program needn't handle non-finite values.
Results may differ from a plain program's by a relative error of at most 0.013.
Values may be sent and summed in bfloat16 or wider, within the bound.
No kernel may reach another device: no remote copies, remote signals or barrier semaphores. Data moves between devices by JAX's collectives and lax.ppermute only.
A program may use at most 192 MiB of HBM per device.

v0:
```python
import jax
import jax.numpy as jnp
from jax import lax
from jax.sharding import PartitionSpec as P


def make_hidden(row_block, gate_blocks, gate_index, up_blocks, up_index):
    row_count = row_block.shape[0]
    block_width = gate_blocks.shape[2]
    split_rows = row_block.reshape(row_count, -1, block_width)
    gate_input = jnp.take(split_rows, gate_index, axis=1)
    up_input = jnp.take(split_rows, up_index, axis=1)
    gate_value = jnp.einsum(
        "rjkc,jkcn->rjn", gate_input, gate_blocks, preferred_element_type=jnp.float32
    )
    up_value = jnp.einsum("rjkc,jkcn->rjn", up_input, up_blocks, preferred_element_type=jnp.float32)
    hidden = (jax.nn.silu(gate_value) * up_value).astype(jnp.bfloat16)
    return hidden.reshape(row_count, -1)


def apply_down(hidden_rows, down_blocks, down_index, block_total):
    row_count = hidden_rows.shape[0]
    column_blocks = down_blocks.shape[0]
    nonzero_count = down_blocks.shape[1]
    block_width = down_blocks.shape[3]
    hidden_split = hidden_rows.reshape(row_count, column_blocks, down_blocks.shape[2])
    products = jnp.einsum(
        "rjn,jknc->rjkc", hidden_split, down_blocks, preferred_element_type=jnp.float32
    )
    flat_products = products.reshape(row_count, column_blocks * nonzero_count, block_width)
    placed = jnp.zeros((row_count, block_total, block_width), jnp.float32)
    placed = placed.at[:, down_index.reshape(-1)].add(flat_products)
    return placed.reshape(row_count, -1)


def body(tokens, row_counts, gate_blocks, gate_index, up_blocks, up_index, down_blocks, down_index):
    own_dp = lax.axis_index("dp")
    own_mp = lax.axis_index("mp")
    rows_in = tokens.shape[0]
    model_width = tokens.shape[1]
    block_total = model_width // down_blocks.shape[3]
    hidden_all = make_hidden(
        lax.all_gather(tokens, "mp", axis=0, tiled=True),
        gate_blocks,
        gate_index,
        up_blocks,
        up_index,
    )
    summed = lax.psum_scatter(
        apply_down(hidden_all, down_blocks, down_index, block_total).astype(jnp.bfloat16),
        "mp",
        scatter_dimension=0,
        tiled=True,
    ).astype(jnp.float32)
    valid_rows = jnp.arange(rows_in, dtype=jnp.int32) < row_counts[own_dp, own_mp]
    return jnp.where(valid_rows[:, None], summed, 0.0).astype(jnp.bfloat16)


def solution(mesh):
    in_specs = (
        P(("dp", "mp"), None),
        P(),
        P("mp", None, None, None),
        P("mp", None),
        P("mp", None, None, None),
        P("mp", None),
        P("mp", None, None, None),
        P("mp", None),
    )
    out_specs = P(("dp", "mp"), None)
    return jax.shard_map(body, mesh=mesh, in_specs=in_specs, out_specs=out_specs, check_vma=False)
```

profile of v0, /device:TPU:0, one launch (start us, length us, event | category | flops | bytes accessed | tf_op | source)
XLA Modules:
  0.0 531.5 jit_solution(15970325136171968062)
XLA Ops:
  6.5 0.0 all-gather.2.cloned.1.call-start
  6.5 0.7 all-gather.2.cloned.1.call-update
  7.3 0.0 reduce-scatter.4.cloned.1.call-start
  7.3 0.8 reshape.48
  8.1 0.7 compare_select_fusion
  8.8 0.1 reshape.83
  8.8 0.7 compare_select_fusion.1
  9.5 0.1 reshape.79
  9.6 0.7 compare_and_fusion
  10.3 0.7 compare_and_fusion.1
  11.0 111.0 %all-gather.2.cloned.1.call-done = bf16[1024,8192]{1,0:T(8,128)(2,1)} async-done(((bf16[64,8192]{1,0:T(8,128)(2,1)}), bf16[1024,8192]{1,0:T(8,128)(2,1)}) %all-gather.2.cloned.1.call-update) | async-done | bytes 16777232 | tf_op jit(solution)/shard_map/all_gather | solution.py:43
  122.0 22.4 %copy.22 = bf16[1024,8192]{0,1:T(8,128)(2,1)} copy(bf16[1024,8192]{1,0:T(8,128)(2,1)} %all-gather.2.cloned.1.call-done) | data formatting | bytes 33554432 | tf_op jit(solution)/shard_map/all_gather | solution.py:43
  144.4 22.4 %copy.23 = bf16[1024,64,128]{2,0,1:T(8,128)(2,1)} copy(bf16[1024,64,128]{0,2,1:T(8,128)(2,1)} %bitcast.53) | data formatting | bytes 33554432 | tf_op jit(solution)/shard_map/reshape | solution.py:10
  166.8 13.3 %gather_fusion.1 = bf16[64,1024,128]{2,1,0:T(8,128)(2,1)} fusion(bf16[1024,64,128]{2,0,1:T(8,128)(2,1)} %copy.23, s32[1024]{0:T(1024)S(1)} %pad_clamp_fusion), kind=kCustom, calls=%fused_computation.1.clone | custom fusion | bytes 33554688 | tf_op jit(solution)/shard_map/jit(_take)/gather | solution.py:12
  180.1 13.4 %gather_fusion = bf16[64,1024,128]{2,1,0:T(8,128)(2,1)} fusion(bf16[1024,64,128]{2,0,1:T(8,128)(2,1)} %copy.23, s32[1024]{0:T(1024)S(1)} %pad_clamp_fusion.1), kind=kCustom, calls=%fused_computation.clone | custom fusion | bytes 33554688 | tf_op jit(solution)/shard_map/jit(_take)/gather | solution.py:11
  193.5 0.0 copy-start
  193.5 10.8 %fusion = f32[4,1024,256,1]{2,1,3,0:T(8,128)} fusion(bf16[4,16,128,256]{3,2,1,0:T(8,128)(2,1)} %param.14, bf16[4,16,1024,128]{3,2,1,0:T(8,128)(2,1)} %bitcast.56, pred[4,16]{1,0:T(4,128)(4,1)S(1)} %compare_and_fusion), kind=kOutput, calls=%fused_computation.3 | convolution fusion | flops 4303355904 | bytes 25165888 | tf_op jit(solution)/shard_map/rjkc,jkcn->rjn/dot_general | solution.py:16
  204.3 2.5 copy-done
  206.7 8.6 %fusion.10 = bf16[1024,4,256]{2,0,1:T(8,128)(2,1)} fusion(f32[4,1024,256,1]{2,1,3,0:T(8,128)} %fusion, bf16[4,16,128,256]{3,2,1,0:T(8,128)(2,1)} %param.12, bf16[4,16,1024,128]{3,2,1,0:T(8,128)(2,1)S(1)} %bitcast.55, pred[4,16]{1,0:T(4,128)(4,1)S(1)} %compare_and_fusion.1), kind=kOutput, calls=%fused_computation.14 | convolution fusion | flops 4309647360 | bytes 27263040 | tf_op jit(solution)/shard_map/rjkc,jkcn->rjn/dot_general | solution.py:13
  215.3 18.4 %fusion.16 = f32[4,1024,16,128]{3,1,2,0:T(8,128)} fusion(bf16[4,16,256,128]{3,2,1,0:T(8,128)(2,1)} %param.16, bf16[1024,4,256]{2,0,1:T(8,128)(2,1)} %fusion.10), kind=kOutput, calls=%fused_computation.20 | convolution fusion | flops 4294967296 | bytes 39845888 | tf_op jit(solution)/shard_map/rjn,jknc->rjkc/dot_general | solution.py:27
  233.8 11.0 %broadcast_in_dim.27 = f32[1024,64,128]{2,0,1:T(8,128)} broadcast(f32[]{:T(128)} %constant.9.clone.1), dimensions={} | broadcast | bytes 33554436 | tf_op jit(solution)/shard_map/broadcast_in_dim | solution.py:31
  244.7 71.2 %scatter_fusion = f32[1024,64,128]{2,0,1:T(8,128)} fusion(f32[1024,64,128]{2,0,1:T(8,128)} %broadcast_in_dim.27, s32[64]{0:T(128)S(1)} %fusion.18, f32[64,1024,128]{2,1,0:T(8,128)} %bitcast.52), kind=kCustom, calls=%fused_computation.2 | custom fusion | flops 8388608 | bytes 100663552 | tf_op jit(solution)/shard_map/scatter-add | solution.py:32
  316.0 17.6 %convert_element_type.16 = bf16[1024,64,128]{2,0,1:T(8,128)(2,1)} convert(f32[1024,64,128]{2,0,1:T(8,128)} %scatter_fusion) | non-fusion elementwise | flops 8388608 | bytes 50331648 | tf_op jit(solution)/shard_map/convert_element_type | solution.py:50
  333.5 22.4 %copy.25 = bf16[1024,64,128]{0,2,1:T(8,128)(2,1)} copy(bf16[1024,64,128]{2,0,1:T(8,128)(2,1)} %convert_element_type.16) | data formatting | bytes 33554432 | tf_op jit(solution)/shard_map/convert_element_type | solution.py:50
  355.9 21.0 %copy.30 = bf16[1024,8192]{1,0:T(8,128)(2,1)} copy(bf16[1024,8192]{0,1:T(8,128)(2,1)} %bitcast.54) | data formatting | bytes 33554432
  377.0 0.0 reduce-scatter.4.cloned.1.call-update
  377.0 1.3 dynamic_slice.3
  378.3 0.6 iota_compare_fusion
  378.9 143.3 %reduce-scatter.4.cloned.1.call-done = bf16[64,8192]{1,0:T(8,128)(2,1)} async-done(((bf16[1024,8192]{1,0:T(8,128)(2,1)}), bf16[64,8192]{1,0:T(8,128)(2,1)}) %reduce-scatter.4.cloned.1.call-update) | async-done | bytes 1048592 | tf_op jit(solution)/shard_map/reduce_scatter | solution.py:49
  522.2 2.4 select_convert_fusion
  (3 shorter events, 0.0 us)
Async XLA Ops:
  6.5 115.5 %all-gather.2.cloned.1.call-start = ((), (), s32[]{:S(2)}) async-start(), calls=%async_computation.1 | async-start | bytes 17825792 | tf_op jit(solution)/shard_map/all_gather | solution.py:43
  7.3 515.0 %reduce-scatter.4.cloned.1.call-start = ((), (), s32[]{:S(2)}) async-start(), calls=%async_computation.2 | async-start | bytes 17825792 | tf_op jit(solution)/shard_map/reduce_scatter | solution.py:49
  193.5 13.3 %copy-start = (bf16[64,1024,128]{2,1,0:T(8,128)(2,1)S(1)}, bf16[64,1024,128]{2,1,0:T(8,128)(2,1)}, u32[]{:S(2)}) copy-start(bf16[64,1024,128]{2,1,0:T(8,128)(2,1)} %gather_fusion) | copy-start | bytes 50331652
Sparse Core Ops, SparseCore 0:
  9.7 112.2 all-gather.1
  377.1 145.0 reduce-scatter.3
where the time goes:
time: 534 us; the launch traced here: 531 us
  waiting for transfers between devices  255 us (48%)
  local copies, waits for them, and re-layouts  131 us (25%)
  other arithmetic  94.6 us (18%)
  matrix products  37.8 us (7%)
  between operations  13.4 us (3%)
    reduce_scatter x1, waiting for transfers between devices, body(): lax.psum_scatter(apply_down(hidden_all, down_blocks, down_index, block_to...  143 us
    all_gather x1, waiting for transfers between devices, body(): lax.all_gather(tokens, 'mp', axis=0, tiled=True)  111 us
    scatter-add x1, other arithmetic, apply_down(): placed = placed.at[:, down_index.reshape(-1)].add(flat_products)  71.2 us
    unnamed x3, local copies, waits for them, and re-layouts  23.5 us
    all_gather x1, local copies, waits for them, and re-layouts, body(): lax.all_gather(tokens, 'mp', axis=0, tiled=True)  22.4 us
    convert_element_type x1, local copies, waits for them, and re-layouts, body(): apply_down(hidden_all, down_blocks, down_index, block_total)  22.4 us
    reshape x1, local copies, waits for them, and re-layouts, make_hidden(): split_rows = row_block.reshape(row_count, -1, block_width)  22.4 us
    dot_general x1, matrix products, apply_down(): jnp.einsum('rjn,jknc->rjkc', hidden_split, down_blocks, preferred_element...  18.4 us
  transfers between devices with their start and end apart: 2, of which 2 were waited for; matrix products, arithmetic and copies ran while one was open for 1% of the time, Pallas kernels for 0%

commit v1 on v0

--- a/solution.py
+++ b/solution.py
@@ -40,7 +40,9 @@
     model_width = tokens.shape[1]
     block_total = model_width // down_blocks.shape[3]
     hidden_all = make_hidden(
-        lax.all_gather(tokens, "mp", axis=0, tiled=True),
+        jnp.concatenate(
+            lax.all_to_all(jnp.stack([tokens] * lax.axis_size("mp")), "mp", 0, 0), axis=0
+        ),
         gate_blocks,
         gate_index,
         up_blocks,

time: 534 us -> 709 us (1.33)
  waiting for transfers between devices: 255 us -> 418 us
  starting transfers between devices: 0.04 us -> 8.06 us
    all_to_all x0 -> x1, waiting for transfers between devices: none -> 270 us  [body(): lax.all_to_all(jnp.stack([tokens] * lax.axis_size('mp')), 'mp', 0, 0)]
    all_gather x1 -> x0, waiting for transfers between devices: 111 us -> none  [body(): lax.all_gather(tokens, 'mp', axis=0, tiled=True)]
    another operation x0 -> x2, local copies, waits for them, and re-layouts: none -> 42.8 us  [the longest x1 36 us: make_hidden(): split_rows = row_block.reshape(row_count, -1, block_width)]
    all_gather x1 -> x0, local copies, waits for them, and re-layouts: 22.4 us -> none  [body(): lax.all_gather(tokens, 'mp', axis=0, tiled=True)]
    reshape x1 -> x0, local copies, waits for them, and re-layouts: 22.4 us -> none  [make_hidden(): split_rows = row_block.reshape(row_count, -1, block_width)]
    unnamed x3 -> x10, local copies, waits for them, and re-layouts: 23.5 us -> 33.5 us
    all_to_all x0 -> x1, starting transfers between devices: none -> 8.02 us  [body(): lax.all_to_all(jnp.stack([tokens] * lax.axis_size('mp')), 'mp', 0, 0)]
  transfers between devices with their start and end apart: 2 -> 2, of which waited for: 2 -> 2; matrix products, arithmetic and copies ran while one was open for 1% -> 0% of each run, Pallas kernels for 0% -> 0%
where the time goes in v1:
time: 709 us; the launch traced here: 707 us
  waiting for transfers between devices  418 us (59%)
  local copies, waits for them, and re-layouts  138 us (19%)
  other arithmetic  91.9 us (13%)
  matrix products  37.8 us (5%)
  between operations  13.5 us (2%)
  starting transfers between devices  8.06 us (1%)
    all_to_all x1, waiting for transfers between devices, body(): lax.all_to_all(jnp.stack([tokens] * lax.axis_size('mp')), 'mp', 0, 0)  270 us
    reduce_scatter x1, waiting for transfers between devices, body(): lax.psum_scatter(apply_down(hidden_all, down_blocks, down_index, block_to...  148 us
    scatter-add x1, other arithmetic, apply_down(): placed = placed.at[:, down_index.reshape(-1)].add(flat_products)  71.3 us
    another operation x1, local copies, waits for them, and re-layouts, make_hidden(): split_rows = row_block.reshape(row_count, -1, block_width)  36 us
    unnamed x10, local copies, waits for them, and re-layouts  33.5 us
    convert_element_type x1, local copies, waits for them, and re-layouts, body(): apply_down(hidden_all, down_blocks, down_index, block_total)  22.4 us
    dot_general x1, matrix products, apply_down(): jnp.einsum('rjn,jknc->rjkc', hidden_split, down_blocks, preferred_element...  18.4 us
    convert_element_type x1, other arithmetic, body(): apply_down(hidden_all, down_blocks, down_index, block_total)  17.5 us
  transfers between devices with their start and end apart: 2, of which 2 were waited for; matrix products, arithmetic and copies ran while one was open for 0% of the time, Pallas kernels for 0%

profile of v1, /device:TPU:0, one launch (start us, length us, event | category | flops | bytes accessed | tf_op | source)
XLA Modules:
  0.0 707.3 jit_solution(2983541110454539969)
XLA Ops:
  6.5 6.8 stack.2
  13.3 0.0 copy-start.3
  13.3 0.0 copy-start.1
  13.3 0.0 copy-start.2
  13.3 8.0 %all-to-all-start = ((bf16[16,64,8192]{2,1,0:T(8,128)(2,1)}), bf16[16,64,8192]{2,1,0:T(8,128)(2,1)}, u32[]{:S(2)}, u32[]{:S(2)}) async-start(bf16[16,64,8192]{2,1,0:T(8,128)(2,1)} %stack.2), calls=%async_computation | async-start | bytes 33554432 | tf_op jit(solution)/shard_map/all_to_all | solution.py:44
  21.4 0.0 reduce-scatter.4.cloned.1.call-start
  21.4 0.0 copy-done.3
  21.4 0.1 reshape.47
  21.5 0.0 copy-done.1
  21.5 0.1 reshape.81
  21.6 0.0 copy-done.2
  21.6 0.1 reshape.77
  21.7 269.9 %all-to-all-done = bf16[16,64,8192]{2,1,0:T(8,128)(2,1)} async-done(((bf16[16,64,8192]{2,1,0:T(8,128)(2,1)}), bf16[16,64,8192]{2,1,0:T(8,128)(2,1)}, u32[]{:S(2)}, u32[]{:S(2)}) %all-to-all-start) | async-done | bytes 16777248 | tf_op jit(solution)/shard_map/all_to_all | solution.py:44
  291.6 9.7 %copy.28 = bf16[128,8,64,128]{3,2,1,0:T(8,128)(2,1)S(1)} copy(bf16[128,8,64,128]{3,1,2,0:T(8,128)(2,1)} %bitcast.25) | data formatting | bytes 33554432
  301.3 36.0 %copy.19 = bf16[1024,64,128]{2,0,1:T(8,128)(2,1)} copy(bf16[1024,64,128]{2,1,0:T(8,128)(2,1)S(1)} %bitcast.55) | data formatting | bytes 33554432 | tf_op jit(solution)/shard_map/reshape;reshape | solution.py:10
  337.3 13.3 %gather_fusion.1 = bf16[64,1024,128]{2,1,0:T(8,128)(2,1)} fusion(bf16[1024,64,128]{2,0,1:T(8,128)(2,1)} %copy.19, s32[1024]{0:T(1024)S(1)} %pad_clamp_fusion), kind=kCustom, calls=%fused_computation.1.clone | custom fusion | bytes 33554688 | tf_op jit(solution)/shard_map/jit(_take)/gather | solution.py:12
  350.6 13.3 %gather_fusion = bf16[64,1024,128]{2,1,0:T(8,128)(2,1)} fusion(bf16[1024,64,128]{2,0,1:T(8,128)(2,1)} %copy.19, s32[1024]{0:T(1024)S(1)} %pad_clamp_fusion.1), kind=kCustom, calls=%fused_computation.clone | custom fusion | bytes 33554688 | tf_op jit(solution)/shard_map/jit(_take)/gather | solution.py:11
  363.9 0.0 copy-start
  363.9 10.8 %fusion = f32[4,1024,256,1]{2,1,3,0:T(8,128)} fusion(bf16[4,16,128,256]{3,2,1,0:T(8,128)(2,1)} %param.14, bf16[4,16,1024,128]{3,2,1,0:T(8,128)(2,1)} %bitcast.58, pred[4,16]{1,0:T(4,128)(4,1)S(1)} %compare_and_fusion), kind=kOutput, calls=%fused_computation.3 | convolution fusion | flops 4303355904 | bytes 25165888 | tf_op jit(solution)/shard_map/rjkc,jkcn->rjn/dot_general | solution.py:16
  374.7 2.4 copy-done
  377.2 8.6 %fusion.10 = bf16[1024,4,256]{2,0,1:T(8,128)(2,1)} fusion(f32[4,1024,256,1]{2,1,3,0:T(8,128)} %fusion, bf16[4,16,128,256]{3,2,1,0:T(8,128)(2,1)} %param.12, bf16[4,16,1024,128]{3,2,1,0:T(8,128)(2,1)S(1)} %bitcast.57, pred[4,16]{1,0:T(4,128)(4,1)S(1)} %compare_and_fusion.1), kind=kOutput, calls=%fused_computation.14 | convolution fusion | flops 4309647360 | bytes 27263040 | tf_op jit(solution)/shard_map/rjkc,jkcn->rjn/dot_general | solution.py:13
  385.7 18.4 %fusion.16 = f32[4,1024,16,128]{3,1,2,0:T(8,128)} fusion(bf16[4,16,256,128]{3,2,1,0:T(8,128)(2,1)} %param.16, bf16[1024,4,256]{2,0,1:T(8,128)(2,1)} %fusion.10), kind=kOutput, calls=%fused_computation.20 | convolution fusion | flops 4294967296 | bytes 39845888 | tf_op jit(solution)/shard_map/rjn,jknc->rjkc/dot_general | solution.py:27
  404.1 11.0 %broadcast_in_dim.27 = f32[1024,64,128]{2,0,1:T(8,128)} broadcast(f32[]{:T(128)} %constant.9.clone.1), dimensions={} | broadcast | bytes 33554436 | tf_op jit(solution)/shard_map/broadcast_in_dim | solution.py:31
  415.1 71.3 %scatter_fusion = f32[1024,64,128]{2,0,1:T(8,128)} fusion(f32[1024,64,128]{2,0,1:T(8,128)} %broadcast_in_dim.27, s32[64]{0:T(128)S(1)} %fusion.18, f32[64,1024,128]{2,1,0:T(8,128)} %bitcast.54), kind=kCustom, calls=%fused_computation.2 | custom fusion | flops 8388608 | bytes 100663552 | tf_op jit(solution)/shard_map/scatter-add | solution.py:32
  486.4 17.5 %convert_element_type.16 = bf16[1024,64,128]{2,0,1:T(8,128)(2,1)} convert(f32[1024,64,128]{2,0,1:T(8,128)} %scatter_fusion) | non-fusion elementwise | flops 8388608 | bytes 50331648 | tf_op jit(solution)/shard_map/convert_element_type | solution.py:52
  503.9 22.4 %copy.21 = bf16[1024,64,128]{0,2,1:T(8,128)(2,1)} copy(bf16[1024,64,128]{2,0,1:T(8,128)(2,1)} %convert_element_type.16) | data formatting | bytes 33554432 | tf_op jit(solution)/shard_map/convert_element_type | solution.py:52
  526.3 21.4 %copy.26 = bf16[1024,8192]{1,0:T(8,128)(2,1)} copy(bf16[1024,8192]{0,1:T(8,128)(2,1)} %bitcast.56) | data formatting | bytes 33554432
  547.7 0.0 reduce-scatter.4.cloned.1.call-update
  547.7 1.3 dynamic_slice.3
  549.0 0.6 iota_compare_fusion
  549.7 148.4 %reduce-scatter.4.cloned.1.call-done = bf16[64,8192]{1,0:T(8,128)(2,1)} async-done(((bf16[1024,8192]{1,0:T(8,128)(2,1)}), bf16[64,8192]{1,0:T(8,128)(2,1)}) %reduce-scatter.4.cloned.1.call-update) | async-done | bytes 1048592 | tf_op jit(solution)/shard_map/reduce_scatter | solution.py:51
  698.1 2.4 select_convert_fusion
  (7 shorter events, 0.0 us)
Async XLA Ops:
  13.3 8.1 %copy-start.3 = (s32[4,16]{1,0:T(4,128)S(1)}, s32[4,16]{1,0:T(4,128)}, u32[]{:S(2)}) copy-start(s32[4,16]{1,0:T(4,128)} %param.17) | copy-start | bytes 772
  13.3 8.2 %copy-start.1 = (s32[4,16]{1,0:T(4,128)S(1)}, s32[4,16]{1,0:T(4,128)}, u32[]{:S(2)}) copy-start(s32[4,16]{1,0:T(4,128)} %param.15) | copy-start | bytes 772
  13.3 8.3 %copy-start.2 = (s32[4,16]{1,0:T(4,128)S(1)}, s32[4,16]{1,0:T(4,128)}, u32[]{:S(2)}) copy-start(s32[4,16]{1,0:T(4,128)} %param.13) | copy-start | bytes 772
  13.3 278.3 %all-to-all-start = ((bf16[16,64,8192]{2,1,0:T(8,128)(2,1)}), bf16[16,64,8192]{2,1,0:T(8,128)(2,1)}, u32[]{:S(2)}, u32[]{:S(2)}) async-start(bf16[16,64,8192]{2,1,0:T(8,128)(2,1)} %stack.2), calls=%async_computation | async-start | bytes 33554432 | tf_op jit(solution)/shard_map/all_to_all | solution.py:44
  21.4 676.7 %reduce-scatter.4.cloned.1.call-start = ((), (), s32[]{:S(2)}) async-start(), calls=%async_computation.2 | async-start | bytes 17825792 | tf_op jit(solution)/shard_map/reduce_scatter | solution.py:51
  363.9 13.3 %copy-start = (bf16[64,1024,128]{2,1,0:T(8,128)(2,1)S(1)}, bf16[64,1024,128]{2,1,0:T(8,128)(2,1)}, u32[]{:S(2)}) copy-start(bf16[64,1024,128]{2,1,0:T(8,128)(2,1)} %gather_fusion) | copy-start | bytes 50331652
Sparse Core Ops, SparseCore 0:
  547.8 150.1 reduce-scatter.3
